TPU v7x, 256 devices: a whole 4x4x8 slice. The times are simulated.
256 devices in a mesh: pop: 32 (over z_hi, x, core), shard: 8 (over z_lo, y).
Axes of the slice: x: 4, y: 4, z: 8 (z_hi: 4, z_lo: 2; z = z_hi * 2 + z_lo), core: 2. Of those that a mesh axis runs over, the one named last changes fastest.
Arguments:
- hidden: bfloat16 [64, 4096, 4096], P('pop', 'shard'), may hold values from -6 to 6
- norm_scale_vector: float32 [4096], replicated, may hold values from 0.3 to 3
- w_value: bfloat16 [4096, 1024], P('shard'), may hold values from -0.09375 to 0.09375
- model_side_factor: bfloat16 [64, 4, 4096], P('pop'), may hold values from -0.09375 to 0.09375
- value_side_factor: bfloat16 [64, 4, 1024], P('pop'), may hold values from -3 to 3
- target: bfloat16 [64, 4096, 1024], P('pop', 'shard'), may hold values from -6 to 6
- lengths: int32 [64], P('pop'), may hold values from 1 to 4096, 163840 in all
- fitness_ranks: int32 [64], replicated, may hold values from 0 to 63, each once
Outputs:
- losses: float32 [64, 4096], P('pop', 'shard')
- scores: float32 [64], P('pop')
- weight_step: bfloat16 [4096, 1024], P('shard')
Inputs may be any that keep to these rules, and one draw needn't show every extreme that they name: Positions t < lengths[m] of member m are live; the lengths of all members sum to 163840, and some member has exactly 4096. `fitness_ranks`: each of 0 to 63 appears once.
All inputs are finite; a program needn't handle non-finite values. No bound on the sum of `lengths` on one device may be relied on, other than what follows from the above.
Results may differ from a plain program's by a relative error of at most 0.0048.
Values may be sent and summed in bfloat16 or wider, within the bound.
A program may use at most 64 MiB of HBM per device.

v0:
```python
import math

import jax
import jax.numpy as jnp
from jax import lax
from jax.sharding import PartitionSpec as P

noise_scale = 0.1
epsilon = 1e-05


def on_device(
    hidden,
    norm_scale_vector,
    w_value,
    model_side_factor,
    value_side_factor,
    target,
    lengths,
    fitness_ranks,
):
    members, span_here, width = hidden.shape
    share, outputs = w_value.shape
    everyone = fitness_ranks.shape[0]
    widened = hidden.astype(jnp.float32)
    inverse = lax.rsqrt(jnp.mean(widened * widened, axis=-1, keepdims=True) + epsilon)
    normalized_input = (widened * inverse * norm_scale_vector).astype(jnp.bfloat16)
    flattened = normalized_input.reshape(members * span_here, width)
    projected = jnp.dot(
        flattened,
        lax.all_gather(w_value, "shard", axis=0, tiled=True),
        preferred_element_type=jnp.float32,
    )
    reduced_output = jnp.einsum(
        "uch,ufh->ucf", normalized_input, model_side_factor, preferred_element_type=jnp.float32
    ).astype(jnp.bfloat16)
    lateral_product = jnp.einsum(
        "nfw,nwx->nfx", reduced_output, value_side_factor, preferred_element_type=jnp.float32
    )
    values = projected.reshape(members, span_here, outputs) + noise_scale * lateral_product
    errors = values - target.astype(jnp.float32)
    squared = jnp.mean(errors * errors, axis=-1)
    first_position = lax.axis_index("shard") * span_here
    position = first_position + lax.broadcasted_iota(jnp.int32, (members, span_here), 1)
    losses = jnp.where(position < lengths[:, None], squared, 0.0)
    totals = lax.psum(jnp.sum(losses, axis=1), "shard")
    scores = totals / lengths.astype(jnp.float32)
    column_start = lax.axis_index("shard") * share
    left_rows = lax.dynamic_slice_in_dim(model_side_factor, column_start, share, 2)
    step_factor = math.sqrt(width) / (noise_scale * everyone)
    own_ranks = lax.dynamic_slice_in_dim(fitness_ranks, lax.axis_index("pop") * members, members, 0)
    own_fitness = own_ranks.astype(jnp.float32) / (everyone - 1) - 0.5
    scaled_left = (left_rows.astype(jnp.float32) * own_fitness[:, None, None]).astype(jnp.bfloat16)
    partial_step = jnp.einsum(
        "mri,mrj->ij", scaled_left, value_side_factor, preferred_element_type=jnp.float32
    )
    summed_step = lax.psum(partial_step, "pop")
    weight_step = (summed_step * step_factor).astype(jnp.bfloat16)
    return (losses, scores, weight_step)


def solution(mesh):
    placed = (
        P("pop", "shard", None),
        P(),
        P("shard", None),
        P("pop", None, None),
        P("pop", None, None),
        P("pop", "shard", None),
        P("pop"),
        P(),
    )
    return jax.shard_map(
        on_device,
        mesh=mesh,
        in_specs=placed,
        out_specs=(P("pop", "shard"), P("pop"), P("shard", None)),
        check_vma=False,
    )
```

profile of v0, /device:TPU:1, one launch (start us, length us, event | category | flops | bytes accessed | tf_op | source)
XLA Modules:
  0.0 409.7 jit_solution(16644616000613431119)
XLA Ops:
  8.0 0.0 copy-start
  8.0 0.0 all-reduce.2.cloned.1.call-start
  8.1 0.7 multiply_add_fusion
  8.8 0.0 copy-done
  8.8 0.0 copy-start.4
  8.8 2.6 convolution_bitcast_fusion
  11.4 0.0 all-reduce.2.cloned.1.call-update
  11.4 0.0 all-gather.2.cloned.1.call-start
  11.4 0.5 all-gather.2.cloned.1.call-update
  12.0 5.1 %fusion = f32[2,512]{1,0:T(2,128)S(1)} fusion(bf16[2,512,4096]{2,1,0:T(8,128)(2,1)} %param.8), kind=kLoop, calls=%fused_computation.2 | loop fusion | flops 12581888 | bytes 8392704 | tf_op jit(solution)/shard_map/reduce_sum | solution.py:26
  17.1 342.5 %all-reduce.2.cloned.1.call-done = f32[512,1024]{1,0:T(8,128)} async-done(((f32[512,1024]{1,0:T(8,128)}), f32[512,1024]{1,0:T(8,128)}) %all-reduce.2.cloned.1.call-update) | async-done | bytes 2097168 | tf_op jit(solution)/shard_map/psum | solution.py:57
  359.6 2.8 multiply_convert_fusion
  362.4 0.0 copy-start.1
  362.4 0.0 copy-start.3
  362.4 0.0 all-gather.2.cloned.1.call-done
  362.4 0.0 copy-done.4
  362.4 15.2 %fusion.3 = f32[2,512,1024]{2,1,0:T(8,128)} fusion(bf16[4096,1024]{1,0:T(8,128)(2,1)} %all-gather.2.cloned.1.call-done, bf16[2,512,4096]{2,1,0:T(8,128)(2,1)} %param.8, f32[4096]{0:T(1024)S(1)} %copy-done.4, f32[2,512]{1,0:T(2,128)S(1)} %add_rsqrt_fusion), kind=kOutput, calls=%fused_computation.5 | convolution fusion | flops 8606711808 | bytes 20992000 | tf_op jit(solution)/shard_map/dot_general | solution.py:29
  377.6 0.0 copy-done.1
  377.6 0.0 copy-done.3
  377.6 0.0 copy-start.2
  377.6 8.0 %multiply_reduce_fusion = f32[2,512]{1,0:T(2,128)S(1)} fusion(bf16[2,512,1024]{2,1,0:T(8,128)(2,1)S(1)} %copy-done.3, f32[2,512,1024]{2,1,0:T(8,128)} %fusion.3, bf16[2,4,1024]{2,1,0:T(4,128)(2,1)S(1)} %copy-done, bf16[2,4,4096]{2,1,0:T(4,128)(2,1)S(1)} %copy-done.1, bf16[2,512,4096]{2,1,0:T(8,128)(2,1)} %param.8, f32[4096]{0:T(1024)S(1)} %copy-done.4, ...), kind=kOutput, calls=%fused_computation.8 | convolution fusion | flops 65014784 | bytes 14786560 | tf_op jit(solution)/shard_map/nfw,nwx->nfx/dot_general | solution.py:37
  385.6 0.0 copy-done.2
  385.7 0.8 fusion.16
  386.4 15.3 %psum.14 = f32[2]{0:T(128)S(1)} all-reduce(f32[2]{0:T(128)S(1)} %get-tuple-element.3), channel_id=1, replica_groups=mesh['pop'=32,'shard'=8] {'shard'}, use_global_device_ids=true, to_apply=%region_3.4 | all-reduce | flops 2 | bytes 16 | tf_op jit(solution)/shard_map/psum | solution.py:46
  401.8 0.5 convert_divide_fusion
  (2 shorter events, 0.0 us)
Async XLA Ops:
  8.0 0.8 copy-start
  8.0 351.6 %all-reduce.2.cloned.1.call-start = ((), (), s32[]{:S(2)}) async-start(), calls=%async_computation.1 | async-start | bytes 4194304 | tf_op jit(solution)/shard_map/psum | solution.py:57
  8.8 353.6 %copy-start.4 = (f32[4096]{0:T(1024)S(1)}, f32[4096]{0:T(1024)}, u32[]{:S(2)}) copy-start(f32[4096]{0:T(1024)} %param.9) | copy-start | bytes 49156
  11.4 351.0 %all-gather.2.cloned.1.call-start = ((), (), s32[]{:S(2)}) async-start(), calls=%async_computation | async-start | bytes 9437184 | tf_op jit(solution)/shard_map/all_gather | solution.py:31
  362.4 15.2 %copy-start.1 = (bf16[2,4,4096]{2,1,0:T(4,128)(2,1)S(1)}, bf16[2,4,4096]{2,1,0:T(4,128)(2,1)}, u32[]{:S(2)}) copy-start(bf16[2,4,4096]{2,1,0:T(4,128)(2,1)} %param.11) | copy-start | bytes 196612
  362.4 15.2 %copy-start.3 = (bf16[2,512,1024]{2,1,0:T(8,128)(2,1)S(1)}, bf16[2,512,1024]{2,1,0:T(8,128)(2,1)}, u32[]{:S(2)}) copy-start(bf16[2,512,1024]{2,1,0:T(8,128)(2,1)} %param.13) | copy-start | bytes 6291460
  377.6 8.0 %copy-start.2 = (s32[2]{0:T(128)S(1)}, s32[2]{0:T(128)}, u32[]{:S(2)}) copy-start(s32[2]{0:T(128)} %param.14) | copy-start | bytes 28
Sparse Core Ops, SparseCore 0:
  11.5 347.9 all-reduce.1
Sparse Core Ops, SparseCore 1:
  13.7 100.5 all-gather.1
where the time goes:
time: 412 us; the launch traced here: 410 us
  waiting for transfers between devices  343 us (83%)
  matrix products  25.8 us (6%)
  between operations  15.5 us (4%)
  blocking collectives  15.3 us (4%)
  other arithmetic  9.94 us (2%)
    psum x1, waiting for transfers between devices, on_device(): summed_step = lax.psum(partial_step, 'pop')  342 us
    psum x1, blocking collectives, on_device(): totals = lax.psum(jnp.sum(losses, axis=1), 'shard')  15.3 us
    dot_general x1, matrix products, on_device(): jnp.dot(flattened, lax.all_gather(w_value, 'shard', axis=0, tiled=True),...  15.2 us
  transfers between devices with their start and end apart: 2, of which 1 were waited for; matrix products, arithmetic and copies ran while one was open for 2% of the time, Pallas kernels for 0%

commit v1 on v0

--- a/solution.py
+++ b/solution.py
@@ -51,10 +51,15 @@
     own_ranks = lax.dynamic_slice_in_dim(fitness_ranks, lax.axis_index("pop") * members, members, 0)
     own_fitness = own_ranks.astype(jnp.float32) / (everyone - 1) - 0.5
     scaled_left = (left_rows.astype(jnp.float32) * own_fitness[:, None, None]).astype(jnp.bfloat16)
-    partial_step = jnp.einsum(
-        "mri,mrj->ij", scaled_left, value_side_factor, preferred_element_type=jnp.float32
+    pack = jnp.concatenate([scaled_left, value_side_factor], axis=2)
+    pack = pack.reshape(pack.shape[0] * pack.shape[1], pack.shape[2])
+    everything = lax.all_gather(pack, "pop", axis=0, tiled=True)
+    summed_step = lax.dot_general(
+        everything[:, :share],
+        everything[:, share:],
+        (((0,), (0,)), ((), ())),
+        preferred_element_type=jnp.float32,
     )
-    summed_step = lax.psum(partial_step, "pop")
     weight_step = (summed_step * step_factor).astype(jnp.bfloat16)
     return (losses, scores, weight_step)
 

time: 412 us -> 162 us (0.39)
  waiting for transfers between devices: 343 us -> 45.7 us
  blocking collectives: 15.3 us -> 66.2 us
    psum x1 -> x0, waiting for transfers between devices: 342 us -> none  [on_device(): summed_step = lax.psum(partial_step, 'pop')]
    all_gather x0 -> x1, blocking collectives: none -> 53.5 us  [on_device(): everything = lax.all_gather(pack, 'pop', axis=0, tiled=True)]
    all_gather x1, waiting for transfers between devices: 0.01 us -> 45 us  [on_device(): lax.all_gather(w_value, 'shard', axis=0, tiled=True)]
  transfers between devices with their start and end apart: 2 -> 1, of which waited for: 1 -> 1; matrix products, arithmetic and copies ran while one was open for 2% -> 6% of each run, Pallas kernels for 0% -> 0%
where the time goes in v1:
time: 162 us; the launch traced here: 159 us
  blocking collectives  66.2 us (41%)
  waiting for transfers between devices  45.7 us (28%)
  matrix products  24.5 us (15%)
  between operations  14.1 us (9%)
  other arithmetic  8.63 us (5%)
    all_gather x1, blocking collectives, on_device(): everything = lax.all_gather(pack, 'pop', axis=0, tiled=True)  53.5 us
    all_gather x1, waiting for transfers between devices, on_device(): lax.all_gather(w_value, 'shard', axis=0, tiled=True)  45 us
    dot_general x1, matrix products, on_device(): jnp.dot(flattened, lax.all_gather(w_value, 'shard', axis=0, tiled=True),...  15.1 us
    psum x1, blocking collectives, on_device(): totals = lax.psum(jnp.sum(losses, axis=1), 'shard')  12.7 us
    dot_general x1, matrix products, on_device(): jnp.einsum('nfw,nwx->nfx', reduced_output, value_side_factor, preferred_e...  8.01 us
    reduce_sum x1, other arithmetic, on_device(): jnp.mean(widened * widened, axis=-1, keepdims=True) + epsilon  5.08 us
  transfers between devices with their start and end apart: 1, of which 1 were waited for; matrix products, arithmetic and copies ran while one was open for 6% of the time, Pallas kernels for 0%

profile of v1, /device:TPU:1, one launch (start us, length us, event | category | flops | bytes accessed | tf_op | source)
XLA Modules:
  0.0 159.2 jit_solution(4412377680226571423)
XLA Ops:
  7.2 0.0 copy-start.4
  7.2 0.0 all-gather.2.cloned.1.call-start
  7.2 0.7 all-gather.2.cloned.1.call-update
  7.9 0.7 multiply_add_fusion
  8.7 0.8 multiply_convert_fusion.1
  9.4 0.7 pad_maximum_fusion
  10.2 5.1 %fusion = f32[2,512]{1,0:T(2,128)S(1)} fusion(bf16[2,512,4096]{2,1,0:T(8,128)(2,1)} %param.8), kind=kLoop, calls=%fused_computation.2 | loop fusion | flops 12581888 | bytes 8392704 | tf_op jit(solution)/shard_map/reduce_sum | solution.py:26
  15.3 53.5 %all_gather.7 = bf16[256,1536]{1,0:T(8,128)(2,1)S(1)} all-gather(bf16[8,1536]{1,0:T(8,128)(2,1)S(1)} %reshape.24), channel_id=1, replica_groups=mesh['pop'=32,'shard'=8] {'pop'}, dimensions={0}, use_global_device_ids=true | all-gather | bytes 811008 | tf_op jit(solution)/shard_map/all_gather | solution.py:56
  68.8 1.4 multiply_convert_fusion
  70.2 0.0 copy-start
  70.2 0.0 copy-start.1
  70.2 0.0 copy-start.3
  70.2 45.0 %all-gather.2.cloned.1.call-done = bf16[4096,1024]{1,0:T(8,128)(2,1)} async-done(((bf16[512,1024]{1,0:T(8,128)(2,1)}), bf16[4096,1024]{1,0:T(8,128)(2,1)}) %all-gather.2.cloned.1.call-update) | async-done | bytes 8388624 | tf_op jit(solution)/shard_map/all_gather | solution.py:31
  115.2 0.0 copy-done.4
  115.2 15.1 %fusion.3 = f32[2,512,1024]{2,1,0:T(8,128)} fusion(bf16[4096,1024]{1,0:T(8,128)(2,1)} %all-gather.2.cloned.1.call-done, bf16[2,512,4096]{2,1,0:T(8,128)(2,1)} %param.8, f32[4096]{0:T(1024)S(1)} %copy-done.4, f32[2,512]{1,0:T(2,128)S(1)} %add_rsqrt_fusion), kind=kOutput, calls=%fused_computation.5 | convolution fusion | flops 8606711808 | bytes 20992000 | tf_op jit(solution)/shard_map/dot_general | solution.py:29
  130.3 0.0 copy-done
  130.3 0.0 copy-done.1
  130.3 0.0 copy-done.3
  130.3 0.0 copy-start.2
  130.3 8.0 %multiply_reduce_fusion = f32[2,512]{1,0:T(2,128)S(1)} fusion(bf16[2,512,1024]{2,1,0:T(8,128)(2,1)S(1)} %copy-done.3, f32[2,512,1024]{2,1,0:T(8,128)} %fusion.3, bf16[2,4,1024]{2,1,0:T(4,128)(2,1)S(1)} %copy-done, bf16[2,4,4096]{2,1,0:T(4,128)(2,1)S(1)} %copy-done.1, bf16[2,512,4096]{2,1,0:T(8,128)(2,1)} %param.8, f32[4096]{0:T(1024)S(1)} %copy-done.4, ...), kind=kOutput, calls=%fused_computation.8 | convolution fusion | flops 65014784 | bytes 14786560 | tf_op jit(solution)/shard_map/nfw,nwx->nfx/dot_general | solution.py:37
  138.3 0.0 copy-done.2
  138.3 0.8 fusion.15
  139.1 12.7 %psum.7 = f32[2]{0:T(128)S(1)} all-reduce(f32[2]{0:T(128)S(1)} %get-tuple-element.3), channel_id=1, replica_groups=mesh['pop'=32,'shard'=8] {'shard'}, use_global_device_ids=true, to_apply=%region_3.4 | all-reduce | flops 2 | bytes 16 | tf_op jit(solution)/shard_map/psum | solution.py:46
  151.8 0.5 convert_divide_fusion
  (3 shorter events, 0.0 us)
Async XLA Ops:
  7.2 108.1 %copy-start.4 = (f32[4096]{0:T(1024)S(1)}, f32[4096]{0:T(1024)}, u32[]{:S(2)}) copy-start(f32[4096]{0:T(1024)} %param.9) | copy-start | bytes 49156
  7.2 108.0 %all-gather.2.cloned.1.call-start = ((), (), s32[]{:S(2)}) async-start(), calls=%async_computation | async-start | bytes 9437184 | tf_op jit(solution)/shard_map/all_gather | solution.py:31
  70.2 60.1 %copy-start = (bf16[2,4,1024]{2,1,0:T(4,128)(2,1)S(1)}, bf16[2,4,1024]{2,1,0:T(4,128)(2,1)}, u32[]{:S(2)}) copy-start(bf16[2,4,1024]{2,1,0:T(4,128)(2,1)} %param.12) | copy-start | bytes 49156
  70.2 60.1 %copy-start.1 = (bf16[2,4,4096]{2,1,0:T(4,128)(2,1)S(1)}, bf16[2,4,4096]{2,1,0:T(4,128)(2,1)}, u32[]{:S(2)}) copy-start(bf16[2,4,4096]{2,1,0:T(4,128)(2,1)} %param.11) | copy-start | bytes 196612
  70.2 60.1 %copy-start.3 = (bf16[2,512,1024]{2,1,0:T(8,128)(2,1)S(1)}, bf16[2,512,1024]{2,1,0:T(8,128)(2,1)}, u32[]{:S(2)}) copy-start(bf16[2,512,1024]{2,1,0:T(8,128)(2,1)} %param.13) | copy-start | bytes 6291460
  130.3 8.0 %copy-start.2 = (s32[2]{0:T(128)S(1)}, s32[2]{0:T(128)}, u32[]{:S(2)}) copy-start(s32[2]{0:T(128)} %param.14) | copy-start | bytes 28
Sparse Core Ops, SparseCore 0:
  9.8 105.3 all-gather.1

commit v2 on v0

v2 whole, which is shorter than its diff:
```python
import math

import jax
import jax.numpy as jnp
from jax import lax
from jax.experimental import pallas as pl
from jax.experimental.pallas import tpu as pltpu
from jax.sharding import PartitionSpec as P

noise_scale = 0.1
epsilon = 1e-05
MESH = pl.DeviceIdType.MESH
NX, NY, NZH, NZL, NC = 4, 4, 4, 2, 2
SHARDS = NZL * NY
POP = NZH * NX * NC


def kernel(
    hidden, gain, weights, left, right, left_in, right_in, target, lengths, ranks,
    losses, scores, step,
    hbuf, nbuf, wbuf, acc, tbuf, abuf, bbuf, fleft, fright, wide_left, wide_right, mine, sums,
    load_sem, send_w, recv_w, send_f, recv_f, send_s, recv_s,
):
    members, span, width = hidden.shape
    share, outputs = weights.shape
    half, quarter = share // 2, share // 4
    pop, shard = lax.axis_index("pop"), lax.axis_index("shard")
    core = lax.rem(pop, NC)
    x = lax.rem(pop // NC, NX)
    zh = pop // (NC * NX)
    zl, y = shard // NY, lax.rem(shard, NY)

    def device(x_, zh_, core_, zl_, y_):
        return (zh_ * (NX * NC) + x_ * NC + core_, zl_ * NY + y_)

    up, down, across = lax.rem(y + 1, NY), lax.rem(y + 3, NY), lax.rem(y + 2, NY)
    other = 1 - zl
    partner = device(x, zh, 1 - core, zl, y)
    y_next, y_prev = device(x, zh, core, zl, up), device(x, zh, core, zl, down)
    z_next = device(x, lax.rem(zh + zl, NZH), core, other, y)
    z_prev = device(x, lax.rem(zh + NZH - other, NZH), core, other, y)
    z_pop = jnp.where(core == 0, z_next[0], z_prev[0])
    z_to = (z_pop, z_next[1])
    z_peers = [device(x, lax.rem(zh + d, NZH), core, zl, y) for d in (1, 2, 3)]
    x_peers = [device(lax.rem(x + d, NX), zh, core, zl, y) for d in (1, 2, 3)]
    shard_peers = [(pop, lax.rem(shard + d, SHARDS)) for d in range(1, SHARDS)]

    own, low_, high, far = zl * NY + y, zl * NY + down, zl * NY + up, zl * NY + across
    own2, low2, high2, far2 = (other * NY + v for v in (y, down, up, across))

    loads = []
    rows = 128
    chunks = members * span // rows
    for j in range(chunks):
        m, q = divmod(j, span // rows)
        loads.append(pltpu.make_async_copy(
            hidden.at[m, pl.ds(q * rows, rows)], hbuf.at[pl.ds(j * rows, rows)], load_sem.at[j]))
    own_load = pltpu.make_async_copy(weights, wbuf.at[own], load_sem.at[chunks])
    slot = core * (NX * NZH) + x * NZH + zh
    columns = pl.ds(pl.multiple_of(shard * share, share), share)
    fl_load = pltpu.make_async_copy(left.at[:, :, columns], fleft.at[slot], load_sem.at[chunks + 1])
    fr_load = pltpu.make_async_copy(right, fright.at[slot], load_sem.at[chunks + 2])
    t_loads = [pltpu.make_async_copy(target.at[m], tbuf.at[pl.ds(m * span, span)],
                                     load_sem.at[chunks + 3 + m]) for m in range(members)]
    for cp in loads + [own_load, fl_load, fr_load] + t_loads:
        cp.start()

    barrier = pltpu.get_barrier_semaphore()
    everyone = [partner, z_next, z_prev] + z_peers + x_peers + shard_peers
    for peer in everyone:
        pl.semaphore_signal(barrier, inc=1, device_id=peer, device_id_type=MESH)
    pl.semaphore_wait(barrier, len(everyone))

    def w_copy(i, src, dst, to):
        return pltpu.make_async_remote_copy(
            src_ref=src, dst_ref=dst, send_sem=send_w.at[i], recv_sem=recv_w.at[i],
            device_id=to, device_id_type=MESH)

    def f_copy(i, src, dst, to):
        return pltpu.make_async_remote_copy(
            src_ref=src, dst_ref=dst, send_sem=send_f.at[i], recv_sem=recv_f.at[i],
            device_id=to, device_id_type=MESH)

    def at(sub):
        return pl.ds(pl.multiple_of(core * half + sub * quarter, quarter), quarter)

    def piece(b, sub):
        return wbuf.at[b, at(sub)]

    def half_of(b, c):
        return wbuf.at[b, pl.ds(pl.multiple_of(c * half, half), half)]

    sent, arrive = {}, {}

    def plan(i, src, dst, landing, to):
        sent[i] = w_copy(i, src, dst, to)
        arrive[i] = w_copy(i, landing, landing, to)

    for i, sub in ((0, 0), (1, 1)):
        plan(i, weights.at[at(sub)], piece(own, sub), piece(low_, sub), y_next)
    plan(2, piece(low_, 0), piece(low_, 0), piece(far, 0), y_next)
    for i, sub in ((3, 1), (4, 0)):
        plan(i, weights.at[at(sub)], piece(own, sub), piece(high, sub), y_prev)
    plan(5, piece(high, 1), piece(high, 1), piece(far, 1), y_prev)
    for i, sub in ((6, 0), (7, 1)):
        plan(i, weights.at[at(sub)], piece(own, sub), piece(own2, sub), z_to)
    for i, b, b2, sub in ((8, low_, low2, 0), (9, high, high2, 1), (10, low_, low2, 1),
                          (11, high, high2, 0), (12, far, far2, 0), (13, far, far2, 1)):
        plan(i, piece(b, sub), piece(b, sub), piece(b2, sub), z_to)
    for i, b in ((14, low_), (15, high), (16, own2), (17, far), (18, low2), (19, high2), (20, far2)):
        plan(i, half_of(b, core), half_of(b, core), half_of(b, 1 - core), partner)

    f_sent = []

    def f_start(i, src, dst, to):
        cp = f_copy(i, src, dst, to)
        cp.start()
        f_sent.append(cp)

    for d in range(3):
        f_start(2 * d, left.at[:, :, columns], fleft.at[slot], z_peers[d])
        f_start(2 * d + 1, right, fright.at[slot], z_peers[d])
    for i in (0, 3, 6, 1, 4, 7):
        sent[i].start()

    for m in range(members):
        pad = jnp.zeros((12, width), jnp.float32)
        a = jnp.concatenate([left_in[m].astype(jnp.float32), pad], axis=0).astype(jnp.bfloat16)
        for b in range(SHARDS):
            abuf[m, b] = a[:, b * share:(b + 1) * share]
        pad = jnp.zeros((12, outputs), jnp.float32)
        bbuf[m] = jnp.concatenate([right_in[m].astype(jnp.float32), pad], axis=0).astype(jnp.bfloat16)

    tile = 16
    for j in range(chunks):
        loads[j].wait()

        def norm(t, carry, j=j):
            r = pl.ds(pl.multiple_of(j * rows + t * tile, tile), tile)
            total = jnp.zeros((tile, share), jnp.float32)
            for b in range(SHARDS):
                v = hbuf[r, b * share:(b + 1) * share].astype(jnp.float32)
                total = total + v * v
            inverse = lax.rsqrt(jnp.sum(total, axis=-1, keepdims=True) / width + epsilon)
            for b in range(SHARDS):
                cols = slice(b * share, (b + 1) * share)
                v = hbuf[r, cols].astype(jnp.float32)
                nbuf[b, r] = (v * inverse * gain[:, cols]).astype(jnp.bfloat16)
            return carry

        lax.fori_loop(0, rows // tile, norm, 0)

    arrive[0].wait_recv()
    sent[2].start()
    sent[8].start()
    arrive[3].wait_recv()
    sent[5].start()
    sent[9].start()

    def f_wait(i, dst):
        f_copy(i, dst, dst, partner).wait_recv()

    for d in range(3):
        back = core * (NX * NZH) + x * NZH + lax.rem(zh + NZH - d - 1, NZH)
        f_wait(2 * d, fleft.at[back])
        f_wait(2 * d + 1, fright.at[back])
    fl_load.wait()
    fr_load.wait()
    group = pl.ds(core * (NX * NZH) + x * NZH, NZH)
    for d in range(3):
        f_start(6 + 2 * d, fleft.at[group], fleft.at[group], x_peers[d])
        f_start(7 + 2 * d, fright.at[group], fright.at[group], x_peers[d])

    for m in range(members):
        r = pl.ds(m * span, span)
        low = jnp.zeros((span, 16), jnp.float32)
        for b in range(SHARDS):
            low = low + lax.dot_general(
                nbuf[b, r], abuf[m, b], (((1,), (1,)), ((), ())), preferred_element_type=jnp.float32)
        low = low.astype(jnp.bfloat16)
        for n in range(0, outputs, 256):
            acc[r, n:n + 256] = noise_scale * jnp.dot(
                low, bbuf[m, :, n:n + 256], preferred_element_type=jnp.float32)

    def multiply(b):
        def body(t, carry):
            c = pl.ds(pl.multiple_of(t * 256, 256), 256)
            acc[:, c] += jnp.dot(nbuf[b], wbuf[b, :, c], preferred_element_type=jnp.float32)
            return carry

        lax.fori_loop(0, outputs // 256, body, 0)

    own_load.wait()
    multiply(own)

    for i in (6, 7):
        arrive[i].wait_recv()
    sent[16].start()
    arrive[1].wait_recv()
    sent[10].start()
    sent[14].start()
    arrive[4].wait_recv()
    sent[11].start()
    sent[15].start()

    for d in range(3):
        g = pl.ds(core * (NX * NZH) + lax.rem(x + NX - d - 1, NX) * NZH, NZH)
        f_wait(6 + 2 * d, fleft.at[g])
        f_wait(7 + 2 * d, fright.at[g])
    mine_f = pl.ds(core * (NX * NZH), NX * NZH)
    f_start(12, fleft.at[mine_f], fleft.at[mine_f], partner)
    f_start(13, fright.at[mine_f], fright.at[mine_f], partner)

    arrive[16].wait_recv()
    multiply(own2)
    arrive[14].wait_recv()
    multiply(low_)
    arrive[2].wait_recv()
    sent[12].start()
    arrive[5].wait_recv()
    sent[13].start()
    sent[17].start()
    arrive[15].wait_recv()
    multiply(high)

    theirs = pl.ds((1 - core) * (NX * NZH), NX * NZH)
    f_wait(12, fleft.at[theirs])
    f_wait(13, fright.at[theirs])
    for k in range(POP):
        c_, rest = divmod(k, NX * NZH)
        x_, zh_ = divmod(rest, NZH)
        first = (zh_ * (NX * NC) + x_ * NC + c_) * members
        for m in range(members):
            r = slice((k * members + m) * 4, (k * members + m) * 4 + 4)
            rank = jnp.full((4, share), ranks[first + m], jnp.int32).astype(jnp.float32)
            fitness = rank / (POP * members - 1) - 0.5
            wide_left[r, :] = fleft[k, m].astype(jnp.float32) * fitness
            wide_right[r, :] = fright[k, m].astype(jnp.float32)
    step_factor = math.sqrt(width) / (noise_scale * POP * members)
    turned = wide_left[...].T.astype(jnp.bfloat16)
    for n in range(0, outputs, 256):
        product = jnp.dot(turned, wide_right[:, n:n + 256].astype(jnp.bfloat16),
                          preferred_element_type=jnp.float32)
        step[:, n:n + 256] = (product * step_factor).astype(jnp.bfloat16)

    arrive[8].wait_recv()
    arrive[10].wait_recv()
    sent[18].start()
    arrive[17].wait_recv()
    multiply(far)
    arrive[9].wait_recv()
    arrive[11].wait_recv()
    sent[19].start()
    arrive[18].wait_recv()
    multiply(low2)
    arrive[12].wait_recv()
    arrive[13].wait_recv()
    sent[20].start()
    arrive[19].wait_recv()
    multiply(high2)
    arrive[20].wait_recv()
    multiply(far2)

    for cp in t_loads:
        cp.wait()
    lanes = lax.broadcasted_iota(jnp.int32, (1, rows), 1)
    partial = []
    for m in range(members):
        running = jnp.zeros((1, rows), jnp.float32)
        for q in range(span // rows):
            r = slice(m * span + q * rows, m * span + (q + 1) * rows)
            part = jnp.zeros((rows, 128), jnp.float32)
            for g in range(0, outputs, 128):
                e = acc[r, g:g + 128] - tbuf[r, g:g + 128].astype(jnp.float32)
                part = part + e * e
            row = jnp.sum(part.T, axis=0, keepdims=True) / outputs
            position = shard * span + q * rows + lanes
            row = jnp.where(position < lengths[m], row, 0.0)
            losses[m:m + 1, q * rows:(q + 1) * rows] = row
            running = running + row
        partial.append(jnp.sum(running, axis=1, keepdims=True))
    which = lax.broadcasted_iota(jnp.int32, (8, 128), 0)
    mine[...] = jnp.where(which == 0, partial[0], partial[1])

    s_sent = []
    for d, peer in enumerate(shard_peers):
        cp = pltpu.make_async_remote_copy(
            src_ref=mine, dst_ref=sums.at[d], send_sem=send_s.at[d], recv_sem=recv_s.at[d],
            device_id=peer, device_id_type=MESH)
        cp.start()
        s_sent.append(cp)
    for i in range(21):
        sent[i].wait_send()
    for cp in f_sent:
        cp.wait_send()
    for cp in s_sent:
        cp.wait()
    whole = jnp.zeros((8, 128), jnp.float32)
    for s in range(SHARDS):
        term = mine[...]
        for d in range(SHARDS - 1):
            term = jnp.where(lax.rem(shard + SHARDS - d - 1, SHARDS) == s, sums[d], term)
        whole = whole + term
    for m in range(members):
        count = jnp.full((8, 128), lengths[m], jnp.int32).astype(jnp.float32)
        scores[m] = (whole / count)[m, 0]


def on_device(hidden, gain, weights, left, right, target, lengths, ranks):
    members, span, width = hidden.shape
    share, outputs = weights.shape
    rank = left.shape[1]
    tokens = members * span
    bf, f32 = jnp.bfloat16, jnp.float32
    hbm = pl.BlockSpec(memory_space=pl.ANY)
    vmem = pl.BlockSpec(memory_space=pltpu.VMEM)
    smem = pl.BlockSpec(memory_space=pltpu.SMEM)
    dma = pltpu.SemaphoreType.DMA
    return tuple(pl.pallas_call(
        kernel,
        out_shape=(
            jax.ShapeDtypeStruct((members, span), f32),
            jax.ShapeDtypeStruct((members,), f32),
            jax.ShapeDtypeStruct((share, outputs), bf),
        ),
        in_specs=[hbm, vmem, hbm, hbm, hbm, vmem, vmem, hbm, smem, smem],
        out_specs=(vmem, smem, vmem),
        scratch_shapes=[
            pltpu.VMEM((tokens, width), bf),
            pltpu.VMEM((SHARDS, tokens, share), bf),
            pltpu.VMEM((SHARDS, share, outputs), bf),
            pltpu.VMEM((tokens, outputs), f32),
            pltpu.VMEM((tokens, outputs), bf),
            pltpu.VMEM((members, SHARDS, 16, share), bf),
            pltpu.VMEM((members, 16, outputs), bf),
            pltpu.VMEM((POP, members, rank, share), bf),
            pltpu.VMEM((POP, members, rank, outputs), bf),
            pltpu.VMEM((POP * members * rank, share), f32),
            pltpu.VMEM((POP * members * rank, outputs), f32),
            pltpu.VMEM((8, 128), f32),
            pltpu.VMEM((SHARDS - 1, 8, 128), f32),
            dma((tokens // 128 + 3 + members,)),
            dma((21,)), dma((21,)), dma((14,)), dma((14,)), dma((7,)), dma((7,)),
        ],
        compiler_params=pltpu.CompilerParams(
            collective_id=0, has_side_effects=True, vmem_limit_bytes=56 * 1024 * 1024),
    )(hidden, gain.reshape(1, width), weights, left, right, left, right, target, lengths, ranks))


def solution(mesh):
    placed = (
        P("pop", "shard", None),
        P(),
        P("shard", None),
        P("pop", None, None),
        P("pop", None, None),
        P("pop", "shard", None),
        P("pop"),
        P(),
    )
    return jax.shard_map(
        on_device,
        mesh=mesh,
        in_specs=placed,
        out_specs=(P("pop", "shard"), P("pop"), P("shard", None)),
        check_vma=False,
    )
```

time: 412 us -> 55.9 us (0.14)
  waiting for transfers between devices: 343 us -> 0 us
  Pallas kernels: 0 us -> 50.4 us
  matrix products: 25.8 us -> 0 us
  blocking collectives: 15.3 us -> 0 us
  between operations: 15.5 us -> 0.64 us
  other arithmetic: 9.94 us -> 0 us
  local copies, waits for them, and re-layouts: 0.02 us -> 4.67 us
    psum x1 -> x0, waiting for transfers between devices: 342 us -> none  [on_device(): summed_step = lax.psum(partial_step, 'pop')]
    pallas_call x0 -> x1, Pallas kernels: none -> 50.4 us  [on_device(): pl.pallas_call(kernel, out_shape=(jax.ShapeDtypeStruct((members, span), f...]
    dot_general x3 -> x0, matrix products: 25.8 us -> none  [the longest x1 15.2 us: on_device(): jnp.dot(flattened, lax.all_gather(w_value, 'shard', axis=0, tiled=True),...]
    psum x1 -> x0, blocking collectives: 15.3 us -> none  [on_device(): totals = lax.psum(jnp.sum(losses, axis=1), 'shard')]
    reduce_sum x2 -> x0, other arithmetic: 5.85 us -> none  [the longest x1 5.08 us: on_device(): jnp.mean(widened * widened, axis=-1, keepdims=True) + epsilon]
    unnamed x10 -> x3, local copies, waits for them, and re-layouts: 0.02 us -> 4.67 us
  transfers between devices with their start and end apart: 2 -> 0, of which waited for: 1 -> 0; matrix products, arithmetic and copies ran while one was open for 2% -> 0% of each run, Pallas kernels for 0% -> 0%
where the time goes in v2:
time: 55.9 us; the launch traced here: 55.7 us
  Pallas kernels  50.4 us (90%)
  local copies, waits for them, and re-layouts  4.67 us (8%)
  between operations  0.64 us (1%)
    pallas_call x1, Pallas kernels, on_device(): pl.pallas_call(kernel, out_shape=(jax.ShapeDtypeStruct((members, span), f...  50.4 us
    unnamed x3, local copies, waits for them, and re-layouts  4.67 us

profile of v2, /device:TPU:1, one launch (start us, length us, event | category | flops | bytes accessed | tf_op | source)
XLA Modules:
  0.0 55.7 jit_solution(4174221063258291998)
XLA Ops:
  0.6 50.4 %shard_map.103 = (f32[2,512]{1,0:T(2,128)}, f32[2]{0:T(128)}, bf16[512,1024]{1,0:T(8,128)(2,1)}) custom-call(bf16[2,512,4096]{2,1,0:T(8,128)(2,1)} %hidden.1, f32[1,4096]{1,0:T(1,128)} %bitcast.1, bf16[512,1024]{1,0:T(8,128)(2,1)} %weights.1, bf16[2,4,4096]{2,1,0:T(4,128)(2,1)} %left_in.1, bf16[2,4,1024]{2,1,0:T(4,128)(2,1)} %right_in.1, ...), custom_call_target="tpu_custom_call" | custom-call | tf_op jit(solution)/shard_map/pallas_call | solution.py:319
  51.0 1.3 %copy.14 = f32[2,512]{1,0:T(2,128)} copy(f32[2,512]{1,0:T(2,128)} %get-tuple-element.6) | data formatting | bytes 8192
  52.3 1.1 %copy.15 = f32[2]{0:T(128)} copy(f32[2]{0:T(128)} %get-tuple-element.7) | data formatting | bytes 16
  53.4 2.3 %copy.16 = bf16[512,1024]{1,0:T(8,128)(2,1)} copy(bf16[512,1024]{1,0:T(8,128)(2,1)} %get-tuple-element.8) | data formatting | bytes 2097152

commit v3 on v2

--- a/solution.py
+++ b/solution.py
@@ -69,6 +69,13 @@
     everyone = [partner, z_next, z_prev] + z_peers + x_peers + shard_peers
     for peer in everyone:
         pl.semaphore_signal(barrier, inc=1, device_id=peer, device_id_type=MESH)
+    for m in range(members):
+        pad = jnp.zeros((12, width), jnp.float32)
+        a = jnp.concatenate([left_in[m].astype(jnp.float32), pad], axis=0).astype(jnp.bfloat16)
+        for b in range(SHARDS):
+            abuf[m, b] = a[:, b * share:(b + 1) * share]
+        pad = jnp.zeros((12, outputs), jnp.float32)
+        bbuf[m] = jnp.concatenate([right_in[m].astype(jnp.float32), pad], axis=0).astype(jnp.bfloat16)
     pl.semaphore_wait(barrier, len(everyone))
 
     def w_copy(i, src, dst, to):
@@ -123,14 +130,6 @@
     for i in (0, 3, 6, 1, 4, 7):
         sent[i].start()
 
-    for m in range(members):
-        pad = jnp.zeros((12, width), jnp.float32)
-        a = jnp.concatenate([left_in[m].astype(jnp.float32), pad], axis=0).astype(jnp.bfloat16)
-        for b in range(SHARDS):
-            abuf[m, b] = a[:, b * share:(b + 1) * share]
-        pad = jnp.zeros((12, outputs), jnp.float32)
-        bbuf[m] = jnp.concatenate([right_in[m].astype(jnp.float32), pad], axis=0).astype(jnp.bfloat16)
-
     tile = 16
     for j in range(chunks):
         loads[j].wait()
@@ -160,6 +159,28 @@
     def f_wait(i, dst):
         f_copy(i, dst, dst, partner).wait_recv()
 
+    for m in range(members):
+        r = pl.ds(m * span, span)
+        low = jnp.zeros((span, 16), jnp.float32)
+        for b in range(SHARDS):
+            low = low + lax.dot_general(
+                nbuf[b, r], abuf[m, b], (((1,), (1,)), ((), ())), preferred_element_type=jnp.float32)
+        low = low.astype(jnp.bfloat16)
+        for n in range(0, outputs, 256):
+            acc[r, n:n + 256] = noise_scale * jnp.dot(
+                low, bbuf[m, :, n:n + 256], preferred_element_type=jnp.float32)
+
+    def multiply(b):
+        def body(t, carry):
+            c = pl.ds(pl.multiple_of(t * 256, 256), 256)
+            acc[:, c] += jnp.dot(nbuf[b], wbuf[b, :, c], preferred_element_type=jnp.float32)
+            return carry
+
+        lax.fori_loop(0, outputs // 256, body, 0)
+
+    own_load.wait()
+    multiply(own)
+
     for d in range(3):
         back = core * (NX * NZH) + x * NZH + lax.rem(zh + NZH - d - 1, NZH)
         f_wait(2 * d, fleft.at[back])
@@ -171,27 +192,6 @@
         f_start(6 + 2 * d, fleft.at[group], fleft.at[group], x_peers[d])
         f_start(7 + 2 * d, fright.at[group], fright.at[group], x_peers[d])
 
-    for m in range(members):
-        r = pl.ds(m * span, span)
-        low = jnp.zeros((span, 16), jnp.float32)
-        for b in range(SHARDS):
-            low = low + lax.dot_general(
-                nbuf[b, r], abuf[m, b], (((1,), (1,)), ((), ())), preferred_element_type=jnp.float32)
-        low = low.astype(jnp.bfloat16)
-        for n in range(0, outputs, 256):
-            acc[r, n:n + 256] = noise_scale * jnp.dot(
-                low, bbuf[m, :, n:n + 256], preferred_element_type=jnp.float32)
-
-    def multiply(b):
-        def body(t, carry):
-            c = pl.ds(pl.multiple_of(t * 256, 256), 256)
-            acc[:, c] += jnp.dot(nbuf[b], wbuf[b, :, c], preferred_element_type=jnp.float32)
-            return carry
-
-        lax.fori_loop(0, outputs // 256, body, 0)
-
-    own_load.wait()
-    multiply(own)
 
     for i in (6, 7):
         arrive[i].wait_recv()
@@ -202,14 +202,6 @@
     arrive[4].wait_recv()
     sent[11].start()
     sent[15].start()
-
-    for d in range(3):
-        g = pl.ds(core * (NX * NZH) + lax.rem(x + NX - d - 1, NX) * NZH, NZH)
-        f_wait(6 + 2 * d, fleft.at[g])
-        f_wait(7 + 2 * d, fright.at[g])
-    mine_f = pl.ds(core * (NX * NZH), NX * NZH)
-    f_start(12, fleft.at[mine_f], fleft.at[mine_f], partner)
-    f_start(13, fright.at[mine_f], fright.at[mine_f], partner)
 
     arrive[16].wait_recv()
     multiply(own2)
@@ -223,6 +215,30 @@
     arrive[15].wait_recv()
     multiply(high)
 
+    for d in range(3):
+        g = pl.ds(core * (NX * NZH) + lax.rem(x + NX - d - 1, NX) * NZH, NZH)
+        f_wait(6 + 2 * d, fleft.at[g])
+        f_wait(7 + 2 * d, fright.at[g])
+    mine_f = pl.ds(core * (NX * NZH), NX * NZH)
+    f_start(12, fleft.at[mine_f], fleft.at[mine_f], partner)
+    f_start(13, fright.at[mine_f], fright.at[mine_f], partner)
+
+
+    arrive[8].wait_recv()
+    arrive[10].wait_recv()
+    sent[18].start()
+    arrive[17].wait_recv()
+    multiply(far)
+    arrive[9].wait_recv()
+    arrive[11].wait_recv()
+    sent[19].start()
+    arrive[18].wait_recv()
+    multiply(low2)
+    arrive[12].wait_recv()
+    arrive[13].wait_recv()
+    sent[20].start()
+    arrive[19].wait_recv()
+    multiply(high2)
     theirs = pl.ds((1 - core) * (NX * NZH), NX * NZH)
     f_wait(12, fleft.at[theirs])
     f_wait(13, fright.at[theirs])
@@ -243,21 +259,6 @@
                           preferred_element_type=jnp.float32)
         step[:, n:n + 256] = (product * step_factor).astype(jnp.bfloat16)
 
-    arrive[8].wait_recv()
-    arrive[10].wait_recv()
-    sent[18].start()
-    arrive[17].wait_recv()
-    multiply(far)
-    arrive[9].wait_recv()
-    arrive[11].wait_recv()
-    sent[19].start()
-    arrive[18].wait_recv()
-    multiply(low2)
-    arrive[12].wait_recv()
-    arrive[13].wait_recv()
-    sent[20].start()
-    arrive[19].wait_recv()
-    multiply(high2)
     arrive[20].wait_recv()
     multiply(far2)
 
@@ -306,6 +307,13 @@
         scores[m] = (whole / count)[m, 0]
 
 
+def settle(losses_in, scores_in, step_in, losses, scores, step):
+    losses[...] = losses_in[...]
+    for m in range(scores.shape[0]):
+        scores[m] = scores_in[m]
+    step[...] = step_in[...]
+
+
 def on_device(hidden, gain, weights, left, right, target, lengths, ranks):
     members, span, width = hidden.shape
     share, outputs = weights.shape
@@ -316,7 +324,7 @@
     vmem = pl.BlockSpec(memory_space=pltpu.VMEM)
     smem = pl.BlockSpec(memory_space=pltpu.SMEM)
     dma = pltpu.SemaphoreType.DMA
-    return tuple(pl.pallas_call(
+    results = pl.pallas_call(
         kernel,
         out_shape=(
             jax.ShapeDtypeStruct((members, span), f32),
@@ -343,8 +351,14 @@
             dma((21,)), dma((21,)), dma((14,)), dma((14,)), dma((7,)), dma((7,)),
         ],
         compiler_params=pltpu.CompilerParams(
-            collective_id=0, has_side_effects=True, vmem_limit_bytes=56 * 1024 * 1024),
-    )(hidden, gain.reshape(1, width), weights, left, right, left, right, target, lengths, ranks))
+            collective_id=0, has_side_effects=True, vmem_limit_bytes=60 * 1024 * 1024),
+    )(hidden, gain.reshape(1, width), weights, left, right, left, right, target, lengths, ranks)
+    return tuple(pl.pallas_call(
+        settle,
+        out_shape=tuple(jax.ShapeDtypeStruct(r.shape, r.dtype) for r in results),
+        in_specs=[vmem, smem, vmem],
+        out_specs=(vmem, smem, vmem),
+    )(*results))
 
 
 def solution(mesh):

time: 55.9 us -> 53.3 us (0.953)
  local copies, waits for them, and re-layouts: 4.67 us -> 0 us
  Pallas kernels: 50.4 us -> 52.4 us
    unnamed x3 -> x0, local copies, waits for them, and re-layouts: 4.67 us -> none
    pallas_call x0 -> x1, Pallas kernels: none -> 2.29 us  [on_device(): pl.pallas_call(settle, out_shape=tuple((jax.ShapeDtypeStruct(r.shape, r.d...]
where the time goes in v3:
time: 53.3 us; the launch traced here: 53 us
  Pallas kernels  52.4 us (98%)
  between operations  0.64 us (1%)
    pallas_call x1, Pallas kernels, on_device(): pl.pallas_call(kernel, out_shape=(jax.ShapeDtypeStruct((members, span), f...  50.1 us
    pallas_call x1, Pallas kernels, on_device(): pl.pallas_call(settle, out_shape=tuple((jax.ShapeDtypeStruct(r.shape, r.d...  2.29 us

profile of v3, /device:TPU:1, one launch (start us, length us, event | category | flops | bytes accessed | tf_op | source)
XLA Modules:
  0.0 53.0 jit_solution(6274308534520083715)
XLA Ops:
  0.6 50.1 %shard_map.103 = (f32[2,512]{1,0:T(2,128)}, f32[2]{0:T(128)}, bf16[512,1024]{1,0:T(8,128)(2,1)}) custom-call(bf16[2,512,4096]{2,1,0:T(8,128)(2,1)} %hidden.1, f32[1,4096]{1,0:T(1,128)} %bitcast.1, bf16[512,1024]{1,0:T(8,128)(2,1)} %weights.1, bf16[2,4,4096]{2,1,0:T(4,128)(2,1)} %left_in.1, bf16[2,4,1024]{2,1,0:T(4,128)(2,1)} %right_in.1, ...), custom_call_target="tpu_custom_call" | custom-call | tf_op jit(solution)/shard_map/pallas_call | solution.py:327
  50.7 2.3 %shard_map.104 = (f32[2,512]{1,0:T(2,128)}, f32[2]{0:T(128)}, bf16[512,1024]{1,0:T(8,128)(2,1)}) custom-call(f32[2,512]{1,0:T(2,128)} %get-tuple-element.6.losses_in, f32[2]{0:T(128)} %get-tuple-element.7.scores_in, bf16[512,1024]{1,0:T(8,128)(2,1)} %get-tuple-element.8.step_in), custom_call_target="tpu_custom_call" | custom-call | tf_op jit(solution)/shard_map/pallas_call | solution.py:356

commit v4 on v3

--- a/solution.py
+++ b/solution.py
@@ -234,11 +234,6 @@
     sent[19].start()
     arrive[18].wait_recv()
     multiply(low2)
-    arrive[12].wait_recv()
-    arrive[13].wait_recv()
-    sent[20].start()
-    arrive[19].wait_recv()
-    multiply(high2)
     theirs = pl.ds((1 - core) * (NX * NZH), NX * NZH)
     f_wait(12, fleft.at[theirs])
     f_wait(13, fright.at[theirs])
@@ -259,6 +254,11 @@
                           preferred_element_type=jnp.float32)
         step[:, n:n + 256] = (product * step_factor).astype(jnp.bfloat16)
 
+    arrive[12].wait_recv()
+    arrive[13].wait_recv()
+    sent[20].start()
+    arrive[19].wait_recv()
+    multiply(high2)
     arrive[20].wait_recv()
     multiply(far2)
 

time: 53.3 us -> 53.4 us (level)
  no operation moved by 1% of the time
where the time goes in v4:
time: 53.4 us; the launch traced here: 53.3 us
  Pallas kernels  52.6 us (99%)
  between operations  0.64 us (1%)
    pallas_call x1, Pallas kernels, on_device(): pl.pallas_call(kernel, out_shape=(jax.ShapeDtypeStruct((members, span), f...  50.4 us
    pallas_call x1, Pallas kernels, on_device(): pl.pallas_call(settle, out_shape=tuple((jax.ShapeDtypeStruct(r.shape, r.d...  2.29 us

profile of v4, /device:TPU:1, one launch (start us, length us, event | category | flops | bytes accessed | tf_op | source)
XLA Modules:
  0.0 53.3 jit_solution(17971613698540521129)
XLA Ops:
  0.6 50.4 %shard_map.103 = (f32[2,512]{1,0:T(2,128)}, f32[2]{0:T(128)}, bf16[512,1024]{1,0:T(8,128)(2,1)}) custom-call(bf16[2,512,4096]{2,1,0:T(8,128)(2,1)} %hidden.1, f32[1,4096]{1,0:T(1,128)} %bitcast.1, bf16[512,1024]{1,0:T(8,128)(2,1)} %weights.1, bf16[2,4,4096]{2,1,0:T(4,128)(2,1)} %left_in.1, bf16[2,4,1024]{2,1,0:T(4,128)(2,1)} %right_in.1, ...), custom_call_target="tpu_custom_call" | custom-call | tf_op jit(solution)/shard_map/pallas_call | solution.py:327
  51.0 2.3 %shard_map.104 = (f32[2,512]{1,0:T(2,128)}, f32[2]{0:T(128)}, bf16[512,1024]{1,0:T(8,128)(2,1)}) custom-call(f32[2,512]{1,0:T(2,128)} %get-tuple-element.6.losses_in, f32[2]{0:T(128)} %get-tuple-element.7.scores_in, bf16[512,1024]{1,0:T(8,128)(2,1)} %get-tuple-element.8.step_in), custom_call_target="tpu_custom_call" | custom-call | tf_op jit(solution)/shard_map/pallas_call | solution.py:356
